TPU v7x, 32 devices: a whole 2x2x4 slice. The times are simulated.
32 devices in a mesh: fsdp: 4 (over y, x), ctx: 2 (over core), tp: 4 (over z).
Axes of the slice: x: 2, y: 2, z: 4, core: 2. Of those that a mesh axis runs over, the one named last changes fastest.
Arguments:
- block_input: float32 [4, 1024, 2048], P('fsdp', 'ctx'), may hold values from -6 to 6
- cotangent: float32 [4, 1024, 2048], P('fsdp', 'ctx'), may hold values from -6 to 6
- w_query: bfloat16 [2048, 2048], P(('fsdp', 'ctx'), 'tp'), may hold values from -0.125 to 0.125
- w_key: bfloat16 [2048, 512], P(('fsdp', 'ctx'), 'tp'), may hold values from -0.125 to 0.125
- w_value: bfloat16 [2048, 512], P(('fsdp', 'ctx'), 'tp'), may hold values from -0.125 to 0.125
- w_output: bfloat16 [2048, 2048], P('tp', ('fsdp', 'ctx')), may hold values from -4 to 4
- w_gate: bfloat16 [2048, 8192], P(('fsdp', 'ctx'), 'tp'), may hold values from -0.125 to 0.125
- w_up: bfloat16 [2048, 8192], P(('fsdp', 'ctx'), 'tp'), may hold values from -0.125 to 0.125
- w_down: bfloat16 [8192, 2048], P('tp', ('fsdp', 'ctx')), may hold values from -0.0625 to 0.0625
- attn_gain: bfloat16 [2048], P(('fsdp', 'ctx')), may hold values from 0.5 to 1.5
- ffn_gain: bfloat16 [2048], P(('fsdp', 'ctx')), may hold values from 0.5 to 1.5
Outputs:
- block_output: float32 [4, 1024, 2048], P('fsdp', 'ctx')
- input_grad: float32 [4, 1024, 2048], P('fsdp', 'ctx')
- grad_query: float32 [2048, 2048], P(('fsdp', 'ctx'), 'tp')
- grad_key: float32 [2048, 512], P(('fsdp', 'ctx'), 'tp')
- grad_value: float32 [2048, 512], P(('fsdp', 'ctx'), 'tp')
- grad_output: float32 [2048, 2048], P('tp', ('fsdp', 'ctx'))
- grad_gate: float32 [2048, 8192], P(('fsdp', 'ctx'), 'tp')
- grad_up: float32 [2048, 8192], P(('fsdp', 'ctx'), 'tp')
- grad_down: float32 [8192, 2048], P('tp', ('fsdp', 'ctx'))
- grad_attn_gain: float32 [2048], P(('fsdp', 'ctx'))
- grad_ffn_gain: float32 [2048], P(('fsdp', 'ctx'))
All inputs are finite; a program needn't handle non-finite values.
Results may differ from a plain program's by a relative error of at most 0.013.
Values may be sent and summed in bfloat16 or wider, within the bound.
No kernel may reach another device: no remote copies, remote signals or barrier semaphores. Data moves between devices by JAX's collectives and lax.ppermute only.
A program may use at most 256 MiB of HBM per device.

v0:
```python
import jax
import jax.numpy as jnp
from jax import lax
from jax.sharding import PartitionSpec as P

HD = 64
EPS = 1e-05
BASE = 500000.0
NEG = -1e30


def shifted(shard, axis, by):
    count = lax.axis_size(axis)
    pairs = [(i, i + by) for i in range(count) if 0 <= i + by < count]
    return lax.ppermute(shard, axis, pairs)


def rotate(values, positions, sign):
    half = values.shape[-1] // 2
    inverse = BASE ** (-(jnp.arange(half, dtype=jnp.float32) * 2.0) / values.shape[-1])
    angle = positions.astype(jnp.float32)[:, None] * inverse[None, :]
    cosine = jnp.cos(angle)[:, None, :]
    sine = sign * jnp.sin(angle)[:, None, :]
    first = values[..., :half]
    second = values[..., half:]
    return jnp.concatenate(
        [first * cosine - second * sine, second * cosine + first * sine], axis=-1
    )


def norm_forward(rows, gain):
    scale = lax.rsqrt(jnp.mean(rows * rows, axis=-1, keepdims=True) + EPS)
    return (rows * scale * gain, scale)


def norm_backward(rows, scale, gain, grad):
    weighted = grad * gain
    d_rows = scale * weighted - rows * scale**3 * jnp.mean(weighted * rows, axis=-1, keepdims=True)
    return (d_rows, jnp.sum(grad * rows * scale, axis=0))


def forward_block(queries, keys, vals, allow, scale):
    scores = jnp.einsum("gbd,kd->gbk", queries, keys, preferred_element_type=jnp.float32) * scale
    scores = jnp.where(allow[None], scores, NEG)
    top = jnp.max(scores, axis=-1, keepdims=True)
    total = top[..., 0] + jnp.log(jnp.sum(jnp.exp(scores - top), axis=-1))
    probs = jnp.exp(scores - total[..., None]).astype(jnp.bfloat16)
    out = jnp.einsum("gbk,kd->gbd", probs, vals, preferred_element_type=jnp.float32)
    return (out.astype(jnp.bfloat16), total)


def backward_block(queries, keys, vals, allow, total, grad_out, out, scale):
    scores = jnp.einsum("gbd,kd->gbk", queries, keys, preferred_element_type=jnp.float32) * scale
    scores = jnp.where(allow[None], scores, NEG)
    probs = jnp.exp(scores - total[..., None])
    rounded = probs.astype(jnp.bfloat16)
    d_vals = jnp.einsum("gbk,gbd->kd", rounded, grad_out, preferred_element_type=jnp.float32)
    d_probs = jnp.einsum("gbd,kd->gbk", grad_out, vals, preferred_element_type=jnp.float32)
    delta = jnp.sum(grad_out.astype(jnp.float32) * out.astype(jnp.float32), axis=-1)
    d_scores = (probs * (d_probs - delta[..., None]) * scale).astype(jnp.bfloat16)
    d_query = jnp.einsum("gbk,kd->gbd", d_scores, keys, preferred_element_type=jnp.float32)
    d_keys = jnp.einsum("gbk,gbd->kd", d_scores, queries, preferred_element_type=jnp.float32)
    return (d_query, d_keys, d_vals)


def split_blocks(tensor, count, block):
    return tensor.reshape((tensor.shape[0], count, block) + tensor.shape[2:]).swapaxes(0, 1)


def attention_forward(grouped, keys, vals, allow, block, scale):

    def per_head(items):
        head_q, head_k, head_v = items
        groups, rows, width = head_q.shape
        count = rows // block
        outs, totals = lax.map(
            lambda piece: forward_block(piece[0], head_k, head_v, piece[1], scale),
            (split_blocks(head_q, count, block), allow.reshape(count, block, allow.shape[1])),
        )
        return (
            outs.swapaxes(0, 1).reshape(groups, rows, width),
            totals.swapaxes(0, 1).reshape(groups, rows),
        )

    return lax.map(per_head, (grouped, keys, vals))


def attention_backward(grouped, keys, vals, allow, totals, grads, outs, block, scale):

    def per_head(items):
        head_q, head_k, head_v, head_t, head_g, head_o = items
        groups, rows, width = head_q.shape
        count = rows // block

        def step(carry, piece):
            d_query, d_keys, d_vals = backward_block(
                piece[0], head_k, head_v, piece[1], piece[2], piece[3], piece[4], scale
            )
            return ((carry[0] + d_keys, carry[1] + d_vals), d_query)

        zeros = jnp.zeros(head_k.shape, jnp.float32)
        pieces = (
            split_blocks(head_q, count, block),
            allow.reshape(count, block, allow.shape[1]),
            split_blocks(head_t, count, block),
            split_blocks(head_g, count, block),
            split_blocks(head_o, count, block),
        )
        (d_keys, d_vals), d_query = lax.scan(step, (zeros, zeros), pieces)
        return (d_query.swapaxes(0, 1).reshape(groups, rows, width), d_keys, d_vals)

    return lax.map(per_head, (grouped, keys, vals, totals, grads, outs))


def dotf(left, right):
    return jnp.dot(left, right, preferred_element_type=jnp.float32)


def body(
    block_input,
    cotangent,
    w_query,
    w_key,
    w_value,
    w_output,
    w_gate,
    w_up,
    w_down,
    attn_gain,
    ffn_gain,
):
    wq, wk, wv, wo, wg, wu, wd, gain_qa, gain_qf = (
        lax.all_gather(w_query, ("fsdp", "ctx"), axis=0, tiled=True),
        lax.all_gather(w_key, ("fsdp", "ctx"), axis=0, tiled=True),
        lax.all_gather(w_value, ("fsdp", "ctx"), axis=0, tiled=True),
        lax.all_gather(w_output, ("fsdp", "ctx"), axis=1, tiled=True),
        lax.all_gather(w_gate, ("fsdp", "ctx"), axis=0, tiled=True),
        lax.all_gather(w_up, ("fsdp", "ctx"), axis=0, tiled=True),
        lax.all_gather(w_down, ("fsdp", "ctx"), axis=1, tiled=True),
        lax.all_gather(attn_gain, ("fsdp", "ctx"), axis=0, tiled=True),
        lax.all_gather(ffn_gain, ("fsdp", "ctx"), axis=0, tiled=True),
    )
    rows = block_input[0]
    cot = cotangent[0]
    local = rows.shape[0]
    block = min(512, local)
    scale = HD ** (-0.5)
    heads = wq.shape[1] // HD
    kv_heads = wk.shape[1] // HD
    groups = heads // kv_heads
    place = lax.axis_index("ctx")
    positions = place * local + jnp.arange(local, dtype=jnp.int32)
    gain_a = gain_qa.astype(jnp.float32)
    gain_f = gain_qf.astype(jnp.float32)
    normed_f, scale_a = norm_forward(rows, gain_a)
    normed = normed_f.astype(jnp.bfloat16)
    query = dotf(normed, wq).reshape(local, heads, HD)
    keys = dotf(normed, wk).reshape(local, kv_heads, HD)
    vals = dotf(normed, wv)
    query_rot = rotate(query, positions, 1.0).astype(jnp.bfloat16)
    keys_rot = rotate(keys, positions, 1.0).astype(jnp.bfloat16).reshape(local, kv_heads * HD)
    vals_b = vals.astype(jnp.bfloat16)
    keys_prev, vals_prev = shifted((keys_rot, vals_b), "ctx", 1)
    all_keys = (
        jnp.concatenate([keys_prev, keys_rot], axis=0)
        .reshape(2 * local, kv_heads, HD)
        .transpose(1, 0, 2)
    )
    all_vals = (
        jnp.concatenate([vals_prev, vals_b], axis=0)
        .reshape(2 * local, kv_heads, HD)
        .transpose(1, 0, 2)
    )
    grouped = query_rot.reshape(local, kv_heads, groups, HD).transpose(1, 2, 0, 3)
    index = jnp.arange(local, dtype=jnp.int32)
    earlier = jnp.broadcast_to(place > 0, (local, local))
    causal = index[None, :] <= index[:, None]
    allow = jnp.concatenate([earlier, causal], axis=1)
    attn, totals = attention_forward(grouped, all_keys, all_vals, allow, block, scale)
    attn_flat = attn.transpose(2, 0, 1, 3).reshape(local, heads * HD)
    hidden = rows + lax.psum(dotf(attn_flat, wo), "tp")
    hnorm_f, scale_f = norm_forward(hidden, gain_f)
    hnorm = hnorm_f.astype(jnp.bfloat16)
    gate = dotf(hnorm, wg)
    up = dotf(hnorm, wu)
    sigma = jax.nn.sigmoid(gate)
    active = gate * sigma
    inner = (active * up).astype(jnp.bfloat16)
    out = hidden + lax.psum(dotf(inner, wd).astype(jnp.bfloat16), "tp").astype(jnp.float32)
    cot_b = cot.astype(jnp.bfloat16)
    d_inner = dotf(cot_b, wd.T)
    d_gate = (d_inner * up * sigma * (1.0 + gate * (1.0 - sigma))).astype(jnp.bfloat16)
    d_up = (d_inner * active).astype(jnp.bfloat16)
    d_hnorm = lax.psum(dotf(d_gate, wg.T) + dotf(d_up, wu.T), "tp")
    d_norm, g_ffn = norm_backward(hidden, scale_f, gain_f, d_hnorm)
    d_hidden = cot + d_norm
    dh_b = d_hidden.astype(jnp.bfloat16)
    d_attn = (
        dotf(dh_b, wo.T)
        .astype(jnp.bfloat16)
        .reshape(local, kv_heads, groups, HD)
        .transpose(1, 2, 0, 3)
    )
    d_query, d_keys, d_vals = attention_backward(
        grouped, all_keys, all_vals, allow, totals, d_attn, attn, block, scale
    )
    keys_grad = d_keys.transpose(1, 0, 2).reshape(2 * local, kv_heads * HD)
    vals_grad = d_vals.transpose(1, 0, 2).reshape(2 * local, kv_heads * HD)
    keys_back, vals_back = shifted((keys_grad[:local], vals_grad[:local]), "ctx", -1)
    keys_own = keys_grad[local:] + keys_back
    vals_own = vals_grad[local:] + vals_back
    d_query = d_query.transpose(2, 0, 1, 3).reshape(local, heads, HD)
    dq_b = rotate(d_query, positions, -1.0).astype(jnp.bfloat16).reshape(local, heads * HD)
    dk_b = (
        rotate(keys_own.reshape(local, kv_heads, HD), positions, -1.0)
        .astype(jnp.bfloat16)
        .reshape(local, kv_heads * HD)
    )
    dv_b = vals_own.astype(jnp.bfloat16)
    d_normed = lax.psum(dotf(dq_b, wq.T) + dotf(dk_b, wk.T) + dotf(dv_b, wv.T), "tp")
    d_rows, g_attn = norm_backward(rows, scale_a, gain_a, d_normed)
    d_input = d_hidden + d_rows
    s_query, s_key, s_value, s_output, s_gate, s_up, s_down, s_attn, s_ffn = (
        lax.psum_scatter(dotf(normed.T, dq_b), ("fsdp", "ctx"), scatter_dimension=0, tiled=True),
        lax.psum_scatter(dotf(normed.T, dk_b), ("fsdp", "ctx"), scatter_dimension=0, tiled=True),
        lax.psum_scatter(dotf(normed.T, dv_b), ("fsdp", "ctx"), scatter_dimension=0, tiled=True),
        lax.psum_scatter(dotf(attn_flat.T, dh_b), ("fsdp", "ctx"), scatter_dimension=1, tiled=True),
        lax.psum_scatter(dotf(hnorm.T, d_gate), ("fsdp", "ctx"), scatter_dimension=0, tiled=True),
        lax.psum_scatter(dotf(hnorm.T, d_up), ("fsdp", "ctx"), scatter_dimension=0, tiled=True),
        lax.psum_scatter(dotf(inner.T, cot_b), ("fsdp", "ctx"), scatter_dimension=1, tiled=True),
        lax.psum_scatter(g_attn, ("fsdp", "ctx"), scatter_dimension=0, tiled=True),
        lax.psum_scatter(g_ffn, ("fsdp", "ctx"), scatter_dimension=0, tiled=True),
    )
    return (
        out[None],
        d_input[None],
        s_query,
        s_key,
        s_value,
        s_output,
        s_gate,
        s_up,
        s_down,
        s_attn,
        s_ffn,
    )


def solution(mesh):
    placed = (
        P("fsdp", "ctx", None),
        P("fsdp", "ctx", None),
        P(("fsdp", "ctx"), "tp"),
        P(("fsdp", "ctx"), "tp"),
        P(("fsdp", "ctx"), "tp"),
        P("tp", ("fsdp", "ctx")),
        P(("fsdp", "ctx"), "tp"),
        P(("fsdp", "ctx"), "tp"),
        P("tp", ("fsdp", "ctx")),
        P(("fsdp", "ctx")),
        P(("fsdp", "ctx")),
    )
    return jax.shard_map(
        body,
        mesh=mesh,
        in_specs=placed,
        out_specs=(
            P("fsdp", "ctx", None),
            P("fsdp", "ctx", None),
            P(("fsdp", "ctx"), "tp"),
            P(("fsdp", "ctx"), "tp"),
            P(("fsdp", "ctx"), "tp"),
            P("tp", ("fsdp", "ctx")),
            P(("fsdp", "ctx"), "tp"),
            P(("fsdp", "ctx"), "tp"),
            P("tp", ("fsdp", "ctx")),
            P(("fsdp", "ctx")),
            P(("fsdp", "ctx")),
        ),
        check_vma=False,
    )
```

profile of v0, /device:TPU:0, one launch (start us, length us, event | category | flops | bytes accessed | tf_op | source)
XLA Modules:
  0.0 1437.5 jit_solution(5688634115593749319)
XLA Ops:
  8.6 10.4 all-gather
  19.0 10.7 all_gather.29
  30.0 3.0 fusion.52
  36.5 2.9 collective-permute-start
  39.4 8.9 all_gather.30
  51.5 2.9 collective-permute-start.1
  55.7 1.7 pad_maximum_fusion
  57.4 1.8 copy.30
  59.2 3.9 copy.28
  63.2 2.9 fusion.65
  66.3 12.7 while.10
  66.3 1.6 fusion.154
  67.9 2.3 exponential_reduce_fusion.2
  70.3 2.3 fusion.155
  72.6 1.6 fusion.154
  74.3 2.3 exponential_reduce_fusion.2
  76.6 2.3 fusion.155
  79.0 4.0 all-gather.10.cloned.1.call-done
  83.0 4.9 fusion.86
  89.7 9.1 all-gather.1
  98.8 144.2 %all-reduce.9.cloned.1.call-done = f32[512,2048]{1,0:T(8,128)} async-done(((f32[512,2048]{1,0:T(8,128)}), f32[512,2048]{1,0:T(8,128)}) %all-reduce.9.cloned.1.call-update) | async-done | bytes 4194320 | tf_op jit(solution)/shard_map/psum | solution.py:181
  243.0 4.0 multiply_reduce_fusion.2
  247.1 2.0 copy-done.1
  249.1 1.7 multiply_convert_fusion.4
  250.8 47.2 %all-gather.12.cloned.1.call-done = bf16[2048,2048]{1,0:T(8,128)(2,1)} async-done(((bf16[256,2048]{1,0:T(8,128)(2,1)}), bf16[2048,2048]{1,0:T(8,128)(2,1)}) %all-gather.12.cloned.1.call-update) | async-done | bytes 8388624 | tf_op jit(solution)/shard_map/all_gather | solution.py:137
  298.0 10.5 fusion.87
  308.6 45.5 %all-gather.14.cloned.1.call-done = bf16[2048,2048]{1,0:T(8,128)(2,1)} async-done(((bf16[256,2048]{1,0:T(8,128)(2,1)}), bf16[2048,2048]{1,0:T(8,128)(2,1)}) %all-gather.14.cloned.1.call-update) | async-done | bytes 8388624 | tf_op jit(solution)/shard_map/all_gather | solution.py:138
  354.1 10.5 fusion.88
  364.6 47.1 %all-gather.16.cloned.1.call-done = bf16[2048,2048]{1,0:T(8,128)(2,1)} async-done(((bf16[2048,256]{1,0:T(8,128)(2,1)}), bf16[2048,2048]{1,0:T(8,128)(2,1)}) %all-gather.16.cloned.1.call-update) | async-done | bytes 8388624 | tf_op jit(solution)/shard_map/all_gather | solution.py:139
  411.7 15.3 %multiply_convert_fusion.1 = (bf16[512,2048]{1,0:T(8,128)(2,1)S(1)}, bf16[512,2048]{1,0:T(8,128)(2,1)}, bf16[512,2048]{1,0:T(8,128)(2,1)}) fusion(f32[512,2048]{1,0:T(8,128)} %fusion.87, f32[512,2048]{1,0:T(8,128)} %fusion.88, bf16[2048,2048]{1,0:T(8,128)(2,1)} %all-gather.16.cloned.1.call-done, f32[1,512,2048]{2,1,0:T(8,128)} %param.16), kind=kOutput, calls=%fused_computation.79 | convolution fusion | flops 4310695936 | bytes 27262976 | tf_op jit(solution)/shard_map/dot_general | solution.py:116
  427.0 8.4 fusion.89
  435.4 6.1 convolution_add_fusion
  441.6 9.8 convolution_convert_fusion
  451.7 145.0 %all-reduce.13.cloned.1.call-done = f32[512,2048]{1,0:T(8,128)} async-done(((f32[512,2048]{1,0:T(8,128)}), f32[512,2048]{1,0:T(8,128)}) %all-reduce.13.cloned.1.call-update) | async-done | bytes 4194320 | tf_op jit(solution)/shard_map/psum | solution.py:194
  596.7 4.5 multiply_reduce_fusion
  601.2 83.0 %all-reduce.11.cloned.1.call-done = bf16[512,2048]{1,0:T(8,128)(2,1)} async-done(((bf16[512,2048]{1,0:T(8,128)(2,1)}), bf16[512,2048]{1,0:T(8,128)(2,1)}) %all-reduce.11.cloned.1.call-update) | async-done | bytes 2097168 | tf_op jit(solution)/shard_map/psum | solution.py:189
  684.2 8.1 bitcast_add_fusion
  692.3 2.0 copy-done.4
  695.6 20.4 %while.27 = (s32[]{:T(128)}, f32[2,4,512,64]{2,3,1,0:T(8,128)}, f32[2,1024,64]{1,2,0:T(8,128)S(1)}, f32[2,1024,64]{1,2,0:T(8,128)}, pred[512,1024]{1,0:T(8,128)(...) while((s32[]{:T(128)}, f32[2,4,512,64]{2,3,1,0:T(8,128)}, ...), condition=%wide.region_12.13_spmd, body=%wide.region_10.12_spmd.sunk | while | flops 1365768192 | bytes 50255028 | solution.py:112
  697.1 3.3 multiply_convert_fusion.7
  702.8 3.1 fusion.170
  707.3 3.3 multiply_convert_fusion.7
  710.6 1.4 fusion.168
  713.0 3.1 fusion.170
  718.6 1.5 collective-permute-start.2
  724.0 2.8 add_add_fusion
  726.8 3.5 fusion.92
  730.4 1.8 fusion.67
  732.2 5.7 fusion.73
  738.0 3.3 fusion.69
  741.4 1.5 copy-done.11
  742.9 9.7 fusion.93
  752.7 9.9 fusion.94
  764.1 10.4 fusion.82
  776.4 105.3 %all-reduce.15.cloned.1.call-done = f32[512,2048]{1,0:T(8,128)} async-done(((f32[512,2048]{1,0:T(8,128)}), f32[512,2048]{1,0:T(8,128)}) %all-reduce.15.cloned.1.call-update) | async-done | bytes 4194320 | tf_op jit(solution)/shard_map/psum | solution.py:220
  881.7 4.5 fusion.61
  886.2 24.1 %all-reduce.3 = (f32[2048]{0:T(1024)S(1)}, f32[2048]{0:T(1024)S(1)}) all-reduce(f32[2048]{0:T(1024)S(1)} %get-tuple-element.169, f32[2048]{0:T(1024)S(1)} %get-tuple-element.167), channel_id=9, replica_groups=mesh['fsdp'=4,'ctx'=2,'tp'=4] {'fsdp','ctx'}, use_global_device_ids=true, to_apply=%region_23.24.clone | all-reduce | flops 4096 | bytes 32768
  911.6 7.8 fusion.58
  920.3 39.8 %reduce-scatter.10.cloned.1.call-done = f32[256,128]{1,0:T(8,128)} async-done(((f32[2048,128]{1,0:T(8,128)}), f32[256,128]{1,0:T(8,128)}) %reduce-scatter.10.cloned.1.call-update) | async-done | bytes 131088 | tf_op jit(solution)/shard_map/reduce_scatter | solution.py:225
  960.1 54.9 %reduce-scatter.14.cloned.1.call-done = f32[512,256]{1,0:T(8,128)} async-done(((f32[512,2048]{1,0:T(8,128)}), f32[512,256]{1,0:T(8,128)}) %reduce-scatter.14.cloned.1.call-update) | async-done | bytes 524304 | tf_op jit(solution)/shard_map/reduce_scatter | solution.py:227
  1015.0 55.1 %reduce-scatter.8.cloned.1.call-done = f32[256,512]{1,0:T(8,128)} async-done(((f32[2048,512]{1,0:T(8,128)}), f32[256,512]{1,0:T(8,128)}) %reduce-scatter.8.cloned.1.call-update) | async-done | bytes 524304 | tf_op jit(solution)/shard_map/reduce_scatter | solution.py:224
  1070.1 120.2 %reduce-scatter.16.cloned.1.call-done = f32[256,2048]{1,0:T(8,128)} async-done(((f32[2048,2048]{1,0:T(8,128)}), f32[256,2048]{1,0:T(8,128)}) %reduce-scatter.16.cloned.1.call-update) | async-done | bytes 2097168 | tf_op jit(solution)/shard_map/reduce_scatter | solution.py:228
  1190.3 120.2 %reduce-scatter.18.cloned.1.call-done = f32[256,2048]{1,0:T(8,128)} async-done(((f32[2048,2048]{1,0:T(8,128)}), f32[256,2048]{1,0:T(8,128)}) %reduce-scatter.18.cloned.1.call-update) | async-done | bytes 2097168 | tf_op jit(solution)/shard_map/reduce_scatter | solution.py:229
  1310.5 120.0 %reduce-scatter.20.cloned.1.call-done = f32[2048,256]{1,0:T(8,128)} async-done(((f32[2048,2048]{1,0:T(8,128)}), f32[2048,256]{1,0:T(8,128)}) %reduce-scatter.20.cloned.1.call-update) | async-done | bytes 2097168 | tf_op jit(solution)/shard_map/reduce_scatter | solution.py:230
  (157 shorter events, 31.0 us)
Async XLA Ops:
  7.2 52.1 %all-gather.8.cloned.1.call-start = ((), (), s32[]{:S(2)}) async-start(), calls=%async_computation.7 | async-start | bytes 2359296 | tf_op jit(solution)/shard_map/all_gather | solution.py:133
  7.9 75.1 %all-gather.10.cloned.1.call-start = ((), (), s32[]{:S(2)}) async-start(), calls=%async_computation.8 | async-start | bytes 2359296 | tf_op jit(solution)/shard_map/all_gather | solution.py:136
  19.0 29.3 %copy-start.20 = (f32[8,1,256]{2,1,0:T(1,128)}, f32[8,1,256]{2,1,0:T(1,128)S(1)}, u32[]{:S(2)}) copy-start(f32[8,1,256]{2,1,0:T(1,128)S(1)} %convert_element_type.149) | copy-start | bytes 24580
  29.7 4.8 copy-start.7
  29.9 4.6 copy-start
  33.5 14.8 %copy-start.23 = (f32[512]{0:T(512)}, f32[512]{0:T(512)S(1)}, u32[]{:S(2)}) copy-start(f32[512]{0:T(512)S(1)} %get-tuple-element.236) | copy-start | bytes 6148
  34.5 31.6 %copy-start.13 = (f32[512,32]{0,1:T(8,128)}, f32[512,32]{0,1:T(8,128)S(1)}, u32[]{:S(2)}) copy-start(f32[512,32]{0,1:T(8,128)S(1)} %get-tuple-element.234) | copy-start | bytes 196612
  34.5 4.9 copy-start.22
  34.9 28.2 %copy-start.2 = (bf16[1,512,2048]{2,1,0:T(8,128)(2,1)}, bf16[1,512,2048]{2,1,0:T(8,128)(2,1)S(1)}, u32[]{:S(2)}) copy-start(bf16[1,512,2048]{2,1,0:T(8,128)(2,1)S(1)} %multiply_convert_fusion.5) | copy-start | bytes 6291460
  36.5 18.2 %collective-permute-start = (bf16[512,128]{0,1:T(8,128)(2,1)}, bf16[512,128]{0,1:T(8,128)(2,1)}, u32[]{:S(2)}, u32[]{:S(2)}) collective-permute-start(bf16[512,128]{0,1:T(8,128)(2,1)} %bitcast.31), channel_id=1, source_target_pairs={{0,4},{1,5},{2,6},{3,7},{8,12},{9,13},{10,14},{11,15},{16,20},{17,... | collective-permute-start | bytes 393224 | tf_op jit(solution)/shard_map/ppermute | solution.py:15
  48.3 3.2 copy-start.9
  48.8 1.4 copy-start.5
  51.5 4.2 collective-permute-start.1
  54.5 188.6 %all-reduce.9.cloned.1.call-start = ((), (), s32[]{:S(2)}) async-start(), calls=%async_computation.9 | async-start | bytes 8388608 | tf_op jit(solution)/shard_map/psum | solution.py:181
  67.9 2.4 copy-start.18
  74.3 2.4 copy-start.18
  87.9 1.8 copy-start.27
  87.9 210.1 %all-gather.12.cloned.1.call-start = ((), (), s32[]{:S(2)}) async-start(), calls=%async_computation.10 | async-start | bytes 9437184 | tf_op jit(solution)/shard_map/all_gather | solution.py:137
  88.5 265.6 %all-gather.14.cloned.1.call-start = ((), (), s32[]{:S(2)}) async-start(), calls=%async_computation.11 | async-start | bytes 9437184 | tf_op jit(solution)/shard_map/all_gather | solution.py:138
  89.1 322.6 %all-gather.16.cloned.1.call-start = ((), (), s32[]{:S(2)}) async-start(), calls=%async_computation.12 | async-start | bytes 9437184 | tf_op jit(solution)/shard_map/all_gather | solution.py:139
  89.7 507.0 %all-reduce.13.cloned.1.call-start = ((), (), s32[]{:S(2)}) async-start(), calls=%async_computation.14 | async-start | bytes 8388608 | tf_op jit(solution)/shard_map/psum | solution.py:194
  247.0 2.0 copy-start.1
  426.9 8.4 copy-start.30
  426.9 8.4 copy-start.26
  441.6 242.6 %all-reduce.11.cloned.1.call-start = ((), (), s32[]{:S(2)}) async-start(), calls=%async_computation.13 | async-start | bytes 4194304 | tf_op jit(solution)/shard_map/psum | solution.py:189
  451.4 430.3 %all-reduce.15.cloned.1.call-start = ((), (), s32[]{:S(2)}) async-start(), calls=%async_computation.15 | async-start | bytes 8388608 | tf_op jit(solution)/shard_map/psum | solution.py:220
  684.2 10.1 copy-start.12
  692.3 2.0 copy-start.4
  692.3 3.3 copy-start.19
  695.6 24.5 %copy-start.14 = (f32[512,32]{0,1:T(8,128)S(1)}, f32[512,32]{0,1:T(8,128)}, u32[]{:S(2)}) copy-start(f32[512,32]{0,1:T(8,128)} %copy-done.13) | copy-start | bytes 196612
  695.6 24.5 %copy-start.17 = (f32[512,32]{0,1:T(8,128)S(1)}, f32[512,32]{0,1:T(8,128)}, u32[]{:S(2)}) copy-start(f32[512,32]{0,1:T(8,128)} %get-tuple-element.232) | copy-start | bytes 196612
  697.0 3.3 copy-start.15
  701.8 1.0 copy-start.16
  707.3 3.3 copy-start.15
  712.0 1.0 copy-start.16
  716.1 5.5 copy-start.6
  717.3 6.5 collective-permute-start.3
  718.6 4.3 collective-permute-start.2
  721.6 1.5 copy-start.8
  722.9 1.0 copy-start.10
  726.8 3.6 copy-start.3
  726.8 193.6 %reduce-scatter.12.cloned.1.call-start = ((), (), s32[]{:S(2)}) async-start(), calls=%async_computation.18 | async-start | bytes 1179648 | tf_op jit(solution)/shard_map/reduce_scatter | solution.py:226
  730.3 229.8 %reduce-scatter.10.cloned.1.call-start = ((), (), s32[]{:S(2)}) async-start(), calls=%async_computation.17 | async-start | bytes 1179648 | tf_op jit(solution)/shard_map/reduce_scatter | solution.py:225
  732.2 282.8 %reduce-scatter.14.cloned.1.call-start = ((), (), s32[]{:S(2)}) async-start(), calls=%async_computation.19 | async-start | bytes 4718592 | tf_op jit(solution)/shard_map/reduce_scatter | solution.py:227
  737.9 332.2 %reduce-scatter.8.cloned.1.call-start = ((), (), s32[]{:S(2)}) async-start(), calls=%async_computation.16 | async-start | bytes 4718592 | tf_op jit(solution)/shard_map/reduce_scatter | solution.py:224
  741.3 1.6 copy-start.11
  741.3 449.0 %reduce-scatter.16.cloned.1.call-start = ((), (), s32[]{:S(2)}) async-start(), calls=%async_computation.20 | async-start | bytes 18874368 | tf_op jit(solution)/shard_map/reduce_scatter | solution.py:228
  752.6 557.9 %reduce-scatter.18.cloned.1.call-start = ((), (), s32[]{:S(2)}) async-start(), calls=%async_computation.21 | async-start | bytes 18874368 | tf_op jit(solution)/shard_map/reduce_scatter | solution.py:229
  762.6 1.6 copy-start.29
  762.6 668.0 %reduce-scatter.20.cloned.1.call-start = ((), (), s32[]{:S(2)}) async-start(), calls=%async_computation.22 | async-start | bytes 18874368 | tf_op jit(solution)/shard_map/reduce_scatter | solution.py:230
  774.5 0.7 copy-start.28
  774.5 107.2 %copy-start.21 = (f32[8,1,256]{2,1,0:T(1,128)S(1)}, f32[8,1,256]{2,1,0:T(1,128)}, u32[]{:S(2)}) copy-start(f32[8,1,256]{2,1,0:T(1,128)} %copy-done.20) | copy-start | bytes 24580
  774.6 107.2 %copy-start.24 = (f32[512]{0:T(512)S(1)}, f32[512]{0:T(512)}, u32[]{:S(2)}) copy-start(f32[512]{0:T(512)} %copy-done.23) | copy-start | bytes 6148
  776.4 135.1 %copy-start.25 = (f32[512]{0:T(512)S(1)}, f32[512]{0:T(512)}, u32[]{:S(2)}) copy-start(f32[512]{0:T(512)} %get-tuple-element.235) | copy-start | bytes 6148
Sparse Core Ops, SparseCore 0:
  9.9 31.1 all-gather.7
  54.6 28.3 all-gather.9
  88.0 154.9 all-reduce.8
  244.8 53.2 all-gather.11
  299.8 54.2 all-gather.13
  355.8 55.8 all-gather.15
  441.7 154.9 all-reduce.12
  599.0 85.0 all-reduce.10
  726.9 154.7 all-reduce.14
  885.3 34.9 reduce-scatter.11
  924.1 35.9 reduce-scatter.9
  963.9 51.0 reduce-scatter.13
  1018.9 51.1 reduce-scatter.7
  1074.1 116.1 reduce-scatter.15
  1194.3 116.1 reduce-scatter.17
  1314.5 115.9 reduce-scatter.19
where the time goes:
time: 1450 us; the launch traced here: 1440 us
  waiting for transfers between devices  1130 us (78%)
  matrix products  149 us (10%)
  blocking collectives  63.1 us (4%)
  other arithmetic  46.2 us (3%)
  local copies, waits for them, and re-layouts  19 us (1%)
  between operations  15.6 us (1%)
    psum x1, waiting for transfers between devices, body(): d_hnorm = lax.psum(dotf(d_gate, wg.T) + dotf(d_up, wu.T), 'tp')  145 us
    psum x1, waiting for transfers between devices, body(): hidden = rows + lax.psum(dotf(attn_flat, wo), 'tp')  144 us
    dot_general x21, matrix products, dotf(): return jnp.dot(left, right, preferred_element_type=jnp.float32)  121 us
    reduce_scatter x1, waiting for transfers between devices, body(): lax.psum_scatter(dotf(hnorm.T, d_gate), ('fsdp', 'ctx'), scatter_dimensio...  120 us
    reduce_scatter x1, waiting for transfers between devices, body(): lax.psum_scatter(dotf(hnorm.T, d_up), ('fsdp', 'ctx'), scatter_dimension=...  120 us
    reduce_scatter x1, waiting for transfers between devices, body(): lax.psum_scatter(dotf(inner.T, cot_b), ('fsdp', 'ctx'), scatter_dimension...  120 us
    psum x1, waiting for transfers between devices, body(): lax.psum(dotf(dq_b, wq.T) + dotf(dk_b, wk.T) + dotf(dv_b, wv.T), 'tp')  105 us
    psum x1, waiting for transfers between devices, body(): lax.psum(dotf(inner, wd).astype(jnp.bfloat16), 'tp').astype(jnp.float32)  83 us
  transfers between devices with their start and end apart: 20, of which 15 were waited for; matrix products, arithmetic and copies ran while one was open for 9% of the time, Pallas kernels for 0%

commit v1 on v0

--- a/solution.py
+++ b/solution.py
@@ -1,3 +1,4 @@
+import functools
 import jax
 import jax.numpy as jnp
 from jax import lax
@@ -7,6 +8,22 @@
 EPS = 1e-05
 BASE = 500000.0
 NEG = -1e30
+
+
+def sources_all_lead(x0, d_out):
+    shares = lax.axis_size(("fsdp", "ctx"))
+    steps_seen = [x0]
+    for d in range(1, shares):
+        res = lax.ppermute(
+            steps_seen[d - 1], ("fsdp", "ctx"), [(t, (t - 1) % shares) for t in range(shares)]
+        )
+        steps_seen.append(res)
+    v_next = jnp.concatenate(steps_seen, d_out)
+    last = lax.axis_index(("fsdp", "ctx"))
+    return jnp.roll(v_next, last * x0.shape[d_out], d_out)
+
+
+cover_spots = functools.partial(sources_all_lead, d_out=0)
 
 
 def shifted(shard, axis, by):
@@ -135,7 +152,7 @@
         lax.all_gather(w_value, ("fsdp", "ctx"), axis=0, tiled=True),
         lax.all_gather(w_output, ("fsdp", "ctx"), axis=1, tiled=True),
         lax.all_gather(w_gate, ("fsdp", "ctx"), axis=0, tiled=True),
-        lax.all_gather(w_up, ("fsdp", "ctx"), axis=0, tiled=True),
+        cover_spots(w_up),
         lax.all_gather(w_down, ("fsdp", "ctx"), axis=1, tiled=True),
         lax.all_gather(attn_gain, ("fsdp", "ctx"), axis=0, tiled=True),
         lax.all_gather(ffn_gain, ("fsdp", "ctx"), axis=0, tiled=True),

time: 1450 us -> 1400 us (0.966)
  waiting for transfers between devices: 1130 us -> 1040 us
  local copies, waits for them, and re-layouts: 19 us -> 46.4 us
  starting transfers between devices: 9.73 us -> 27.5 us
    psum x1, waiting for transfers between devices: 144 us -> 26 us  [body(): hidden = rows + lax.psum(dotf(attn_flat, wo), 'tp')]
    ppermute x0 -> x7, waiting for transfers between devices: none -> 66.3 us  [sources_all_lead(): lax.ppermute(steps_seen[d - 1], ('fsdp', 'ctx'), [(t, (t - 1) % shares) f...]
    all_gather x1 -> x0, waiting for transfers between devices: 45.5 us -> none  [body(): lax.all_gather(w_up, ('fsdp', 'ctx'), axis=0, tiled=True)]
    unnamed x61 -> x98, local copies, waits for them, and re-layouts: 11.5 us -> 37.9 us
    ppermute x0 -> x7, starting transfers between devices: none -> 17.6 us  [sources_all_lead(): lax.ppermute(steps_seen[d - 1], ('fsdp', 'ctx'), [(t, (t - 1) % shares) f...]
  transfers between devices with their start and end apart: 20 -> 26, of which waited for: 15 -> 20; matrix products, arithmetic and copies ran while one was open for 9% -> 11% of each run, Pallas kernels for 0% -> 0%
where the time goes in v1:
time: 1400 us; the launch traced here: 1390 us
  waiting for transfers between devices  1040 us (74%)
  matrix products  149 us (11%)
  blocking collectives  70.3 us (5%)
  local copies, waits for them, and re-layouts  46.4 us (3%)
  other arithmetic  46.2 us (3%)
  starting transfers between devices  27.5 us (2%)
  between operations  15.6 us (1%)
    psum x1, waiting for transfers between devices, body(): d_hnorm = lax.psum(dotf(d_gate, wg.T) + dotf(d_up, wu.T), 'tp')  145 us
    dot_general x21, matrix products, dotf(): return jnp.dot(left, right, preferred_element_type=jnp.float32)  121 us
    reduce_scatter x1, waiting for transfers between devices, body(): lax.psum_scatter(dotf(hnorm.T, d_gate), ('fsdp', 'ctx'), scatter_dimensio...  120 us
    reduce_scatter x1, waiting for transfers between devices, body(): lax.psum_scatter(dotf(hnorm.T, d_up), ('fsdp', 'ctx'), scatter_dimension=...  120 us
    reduce_scatter x1, waiting for transfers between devices, body(): lax.psum_scatter(dotf(inner.T, cot_b), ('fsdp', 'ctx'), scatter_dimension...  120 us
    psum x1, waiting for transfers between devices, body(): lax.psum(dotf(dq_b, wq.T) + dotf(dk_b, wk.T) + dotf(dv_b, wv.T), 'tp')  105 us
    psum x1, waiting for transfers between devices, body(): lax.psum(dotf(inner, wd).astype(jnp.bfloat16), 'tp').astype(jnp.float32)  83 us
    ppermute x7, waiting for transfers between devices, sources_all_lead(): lax.ppermute(steps_seen[d - 1], ('fsdp', 'ctx'), [(t, (t - 1) % shares) f...  66.3 us
  transfers between devices with their start and end apart: 26, of which 20 were waited for; matrix products, arithmetic and copies ran while one was open for 11% of the time, Pallas kernels for 0%

profile of v1, /device:TPU:0, one launch (start us, length us, event | category | flops | bytes accessed | tf_op | source)
XLA Modules:
  0.0 1392.5 jit_solution(15430772283138234099)
XLA Ops:
  8.6 10.4 all-gather
  19.0 10.7 all_gather.26
  30.0 3.0 fusion.56
  36.5 2.9 collective-permute-start
  39.4 8.9 all_gather.27
  51.5 2.9 collective-permute-start.1
  59.2 3.9 copy.28
  63.1 2.9 fusion.72
  66.2 12.7 while.10
  67.9 2.3 exponential_reduce_fusion.2
  74.2 2.3 exponential_reduce_fusion.2
  78.9 4.0 all-gather.9.cloned.1.call-done
  83.0 4.9 fusion.96
  90.7 12.3 collective-permute-done.2
  104.0 3.2 collective-permute-start.3
  107.2 12.3 collective-permute-done.3
  120.5 3.2 collective-permute-start.4
  123.7 12.3 collective-permute-done.4
  137.0 3.2 collective-permute-start.5
  140.2 12.3 collective-permute-done.5
  153.5 3.2 collective-permute-start.6
  156.7 12.3 collective-permute-done.6
  169.0 2.9 collective-permute-start.7
  171.9 16.3 %all-gather.1 = bf16[8,1,256]{2,1,0:T(2,128)(2,1)S(1)} all-gather(bf16[1,1,256]{2,1,0:T(2,128)(2,1)S(1)} %reshape.299), channel_id=1, replica_groups=mesh['fsdp'=4,'ctx'=2,'tp'=4] {'fsdp','ctx'}, dimensions={0}, use_global_device_ids=true | all-gather | bytes 4608 | tf_op jit(solution)/shard_map/all_gather | solution.py:158
  189.3 2.6 constant_dynamic-update-slice_fusion.14
  195.6 2.4 constant_dynamic-update-slice_fusion.10
  200.3 4.7 collective-permute-done.8
  213.7 2.3 constant_dynamic-update-slice_fusion.1
  217.1 26.0 %all-reduce.9.cloned.1.call-done = f32[512,2048]{1,0:T(8,128)} async-done(((f32[512,2048]{1,0:T(8,128)}), f32[512,2048]{1,0:T(8,128)}) %all-reduce.9.cloned.1.call-update) | async-done | bytes 4194320 | tf_op jit(solution)/shard_map/psum | solution.py:198
  243.0 4.0 multiply_reduce_fusion.2
  250.8 47.2 %all-gather.11.cloned.1.call-done = bf16[2048,2048]{1,0:T(8,128)(2,1)} async-done(((bf16[256,2048]{1,0:T(8,128)(2,1)}), bf16[2048,2048]{1,0:T(8,128)(2,1)}) %all-gather.11.cloned.1.call-update) | async-done | bytes 8388624 | tf_op jit(solution)/shard_map/all_gather | solution.py:154
  298.0 10.6 fusion.97
  308.6 47.0 %all-gather.13.cloned.1.call-done = bf16[2048,2048]{1,0:T(8,128)(2,1)} async-done(((bf16[2048,256]{1,0:T(8,128)(2,1)}), bf16[2048,2048]{1,0:T(8,128)(2,1)}) %all-gather.13.cloned.1.call-update) | async-done | bytes 8388624 | tf_op jit(solution)/shard_map/all_gather | solution.py:156
  355.7 11.3 fusion.90
  367.0 12.6 multiply_convert_fusion.1
  379.7 6.9 fusion.98
  386.6 9.8 fusion.67
  396.4 9.8 convolution_convert_fusion
  406.5 145.0 %all-reduce.13.cloned.1.call-done = f32[512,2048]{1,0:T(8,128)} async-done(((f32[512,2048]{1,0:T(8,128)}), f32[512,2048]{1,0:T(8,128)}) %all-reduce.13.cloned.1.call-update) | async-done | bytes 4194320 | tf_op jit(solution)/shard_map/psum | solution.py:211
  551.6 4.5 multiply_reduce_fusion
  556.1 83.0 %all-reduce.11.cloned.1.call-done = bf16[512,2048]{1,0:T(8,128)(2,1)} async-done(((bf16[512,2048]{1,0:T(8,128)(2,1)}), bf16[512,2048]{1,0:T(8,128)(2,1)}) %all-reduce.11.cloned.1.call-update) | async-done | bytes 2097168 | tf_op jit(solution)/shard_map/psum | solution.py:206
  639.1 8.1 bitcast_add_fusion
  650.5 20.4 %while.27 = (s32[]{:T(128)}, f32[2,4,512,64]{2,3,1,0:T(8,128)}, f32[2,1024,64]{1,2,0:T(8,128)S(1)}, f32[2,1024,64]{1,2,0:T(8,128)}, pred[512,1024]{1,0:T(8,128)(...) while((s32[]{:T(128)}, f32[2,4,512,64]{2,3,1,0:T(8,128)}, ...), condition=%wide.region_12.13_spmd, body=%wide.region_10.12_spmd.sunk | while | flops 1365768192 | bytes 50255028 | solution.py:129
  651.9 3.3 multiply_convert_fusion.7
  657.6 3.1 fusion.177
  662.2 3.3 multiply_convert_fusion.7
  667.8 3.1 fusion.177
  678.8 2.8 add_add_fusion
  681.7 3.5 fusion.101
  687.0 5.7 fusion.80
  692.8 3.3 fusion.76
  697.7 9.8 fusion.102
  707.6 9.9 fusion.103
  719.1 10.4 fusion.92
  731.4 105.1 %all-reduce.15.cloned.1.call-done = f32[512,2048]{1,0:T(8,128)} async-done(((f32[512,2048]{1,0:T(8,128)}), f32[512,2048]{1,0:T(8,128)}) %all-reduce.15.cloned.1.call-update) | async-done | bytes 4194320 | tf_op jit(solution)/shard_map/psum | solution.py:237
  836.5 4.5 fusion.65
  841.0 24.1 %all-reduce.3 = (f32[2048]{0:T(1024)S(1)}, f32[2048]{0:T(1024)S(1)}) all-reduce(f32[2048]{0:T(1024)S(1)} %get-tuple-element.169, f32[2048]{0:T(1024)S(1)} %get-tuple-element.167), channel_id=9, replica_groups=mesh['fsdp'=4,'ctx'=2,'tp'=4] {'fsdp','ctx'}, use_global_device_ids=true, to_apply=%region_23.24.clone | all-reduce | flops 4096 | bytes 32768
  866.4 7.8 fusion.62
  875.3 39.6 %reduce-scatter.10.cloned.1.call-done = f32[256,128]{1,0:T(8,128)} async-done(((f32[2048,128]{1,0:T(8,128)}), f32[256,128]{1,0:T(8,128)}) %reduce-scatter.10.cloned.1.call-update) | async-done | bytes 131088 | tf_op jit(solution)/shard_map/reduce_scatter | solution.py:242
  914.9 55.0 %reduce-scatter.14.cloned.1.call-done = f32[512,256]{1,0:T(8,128)} async-done(((f32[512,2048]{1,0:T(8,128)}), f32[512,256]{1,0:T(8,128)}) %reduce-scatter.14.cloned.1.call-update) | async-done | bytes 524304 | tf_op jit(solution)/shard_map/reduce_scatter | solution.py:244
  969.9 55.0 %reduce-scatter.8.cloned.1.call-done = f32[256,512]{1,0:T(8,128)} async-done(((f32[2048,512]{1,0:T(8,128)}), f32[256,512]{1,0:T(8,128)}) %reduce-scatter.8.cloned.1.call-update) | async-done | bytes 524304 | tf_op jit(solution)/shard_map/reduce_scatter | solution.py:241
  1024.9 120.4 %reduce-scatter.16.cloned.1.call-done = f32[256,2048]{1,0:T(8,128)} async-done(((f32[2048,2048]{1,0:T(8,128)}), f32[256,2048]{1,0:T(8,128)}) %reduce-scatter.16.cloned.1.call-update) | async-done | bytes 2097168 | tf_op jit(solution)/shard_map/reduce_scatter | solution.py:245
  1145.3 120.2 %reduce-scatter.18.cloned.1.call-done = f32[256,2048]{1,0:T(8,128)} async-done(((f32[2048,2048]{1,0:T(8,128)}), f32[256,2048]{1,0:T(8,128)}) %reduce-scatter.18.cloned.1.call-update) | async-done | bytes 2097168 | tf_op jit(solution)/shard_map/reduce_scatter | solution.py:246
  1265.5 120.0 %reduce-scatter.20.cloned.1.call-done = f32[2048,256]{1,0:T(8,128)} async-done(((f32[2048,2048]{1,0:T(8,128)}), f32[2048,256]{1,0:T(8,128)}) %reduce-scatter.20.cloned.1.call-update) | async-done | bytes 2097168 | tf_op jit(solution)/shard_map/reduce_scatter | solution.py:247
  (207 shorter events, 76.1 us)
Async XLA Ops:
  7.2 52.0 %all-gather.7.cloned.1.call-start = ((), (), s32[]{:S(2)}) async-start(), calls=%async_computation.7 | async-start | bytes 2359296 | tf_op jit(solution)/shard_map/all_gather | solution.py:150
  7.9 75.1 %all-gather.9.cloned.1.call-start = ((), (), s32[]{:S(2)}) async-start(), calls=%async_computation.8 | async-start | bytes 2359296 | tf_op jit(solution)/shard_map/all_gather | solution.py:153
  19.0 29.3 %copy-start.30 = (f32[8,1,256]{2,1,0:T(1,128)}, f32[8,1,256]{2,1,0:T(1,128)S(1)}, u32[]{:S(2)}) copy-start(f32[8,1,256]{2,1,0:T(1,128)S(1)} %convert_element_type.149) | copy-start | bytes 24580
  29.7 4.8 copy-start.7
  29.9 4.6 copy-start
  33.5 14.8 %copy-start.33 = (f32[512]{0:T(512)}, f32[512]{0:T(512)S(1)}, u32[]{:S(2)}) copy-start(f32[512]{0:T(512)S(1)} %get-tuple-element.236) | copy-start | bytes 6148
  34.5 31.5 %copy-start.23 = (f32[512,32]{0,1:T(8,128)}, f32[512,32]{0,1:T(8,128)S(1)}, u32[]{:S(2)}) copy-start(f32[512,32]{0,1:T(8,128)S(1)} %get-tuple-element.234) | copy-start | bytes 196612
  34.5 4.9 copy-start.32
  34.9 28.2 %copy-start.2 = (bf16[1,512,2048]{2,1,0:T(8,128)(2,1)}, bf16[1,512,2048]{2,1,0:T(8,128)(2,1)S(1)}, u32[]{:S(2)}) copy-start(bf16[1,512,2048]{2,1,0:T(8,128)(2,1)S(1)} %multiply_convert_fusion.5) | copy-start | bytes 6291460
  36.5 18.2 %collective-permute-start = (bf16[512,128]{0,1:T(8,128)(2,1)}, bf16[512,128]{0,1:T(8,128)(2,1)}, u32[]{:S(2)}, u32[]{:S(2)}) collective-permute-start(bf16[512,128]{0,1:T(8,128)(2,1)} %bitcast.31), channel_id=1, source_target_pairs={{0,4},{1,5},{2,6},{3,7},{8,12},{9,13},{10,14},{11,15},{16,20},{17,... | collective-permute-start | bytes 393224 | tf_op jit(solution)/shard_map/ppermute | solution.py:32
  48.3 3.2 copy-start.9
  48.8 1.4 copy-start.5
  51.5 4.2 collective-permute-start.1
  54.4 188.6 %all-reduce.9.cloned.1.call-start = ((), (), s32[]{:S(2)}) async-start(), calls=%async_computation.9 | async-start | bytes 8388608 | tf_op jit(solution)/shard_map/psum | solution.py:198
  67.9 2.4 copy-start.28
  74.2 2.4 copy-start.28
  87.9 1.5 copy-start.11
  87.9 84.0 %copy-start.36 = (bf16[256]{0:T(256)(128)(2,1)S(1)}, bf16[256]{0:T(256)(128)(2,1)}, u32[]{:S(2)}) copy-start(bf16[256]{0:T(256)(128)(2,1)} %param.25) | copy-start | bytes 1540
  87.9 210.1 %all-gather.11.cloned.1.call-start = ((), (), s32[]{:S(2)}) async-start(), calls=%async_computation.10 | async-start | bytes 9437184 | tf_op jit(solution)/shard_map/all_gather | solution.py:154
  88.5 267.2 %all-gather.13.cloned.1.call-start = ((), (), s32[]{:S(2)}) async-start(), calls=%async_computation.11 | async-start | bytes 9437184 | tf_op jit(solution)/shard_map/all_gather | solution.py:156
  89.1 462.5 %all-reduce.13.cloned.1.call-start = ((), (), s32[]{:S(2)}) async-start(), calls=%async_computation.13 | async-start | bytes 8388608 | tf_op jit(solution)/shard_map/psum | solution.py:211
  89.3 13.7 collective-permute-start.2
  104.0 15.5 %collective-permute-start.3 = (bf16[256,2048]{1,0:T(8,128)(2,1)S(1)}, bf16[256,2048]{1,0:T(8,128)(2,1)S(1)}, u32[]{:S(2)}, u32[]{:S(2)}) collective-permute-start(bf16[256,2048]{1,0:T(8,128)(2,1)S(1)} %collective-permute-done.2), channel_id=1, source_target_pairs={{0,28},{4,0},{8,4},{12,8},{16,12},{20,16},{24,20},{28,24},{1,29},{... | collective-permute-start | bytes 3145736 | tf_op jit(solution)/shard_map/ppermute | solution.py:17
  120.5 15.5 %collective-permute-start.4 = (bf16[256,2048]{1,0:T(8,128)(2,1)S(1)}, bf16[256,2048]{1,0:T(8,128)(2,1)S(1)}, u32[]{:S(2)}, u32[]{:S(2)}) collective-permute-start(bf16[256,2048]{1,0:T(8,128)(2,1)S(1)} %collective-permute-done.3), channel_id=1, source_target_pairs={{0,28},{4,0},{8,4},{12,8},{16,12},{20,16},{24,20},{28,24},{1,29},{... | collective-permute-start | bytes 3145736 | tf_op jit(solution)/shard_map/ppermute | solution.py:17
  137.0 15.5 %collective-permute-start.5 = (bf16[256,2048]{1,0:T(8,128)(2,1)S(1)}, bf16[256,2048]{1,0:T(8,128)(2,1)S(1)}, u32[]{:S(2)}, u32[]{:S(2)}) collective-permute-start(bf16[256,2048]{1,0:T(8,128)(2,1)S(1)} %collective-permute-done.4), channel_id=1, source_target_pairs={{0,28},{4,0},{8,4},{12,8},{16,12},{20,16},{24,20},{28,24},{1,29},{... | collective-permute-start | bytes 3145736 | tf_op jit(solution)/shard_map/ppermute | solution.py:17
  153.5 15.5 %collective-permute-start.6 = (bf16[256,2048]{1,0:T(8,128)(2,1)S(1)}, bf16[256,2048]{1,0:T(8,128)(2,1)}, u32[]{:S(2)}, u32[]{:S(2)}) collective-permute-start(bf16[256,2048]{1,0:T(8,128)(2,1)S(1)} %collective-permute-done.5), channel_id=1, source_target_pairs={{0,28},{4,0},{8,4},{12,8},{16,12},{20,16},{24,20},{28,24},{1,29},{... | collective-permute-start | bytes 3145736 | tf_op jit(solution)/shard_map/ppermute | solution.py:17
  169.0 22.9 %collective-permute-start.7 = (bf16[256,2048]{1,0:T(8,128)(2,1)}, bf16[256,2048]{1,0:T(8,128)(2,1)}, u32[]{:S(2)}, u32[]{:S(2)}) collective-permute-start(bf16[256,2048]{1,0:T(8,128)(2,1)} %collective-permute-done.6), channel_id=1, source_target_pairs={{0,28},{4,0},{8,4},{12,8},{16,12},{20,16},{24,20},{28,24},{1,29},{... | collective-permute-start | bytes 3145736 | tf_op jit(solution)/shard_map/ppermute | solution.py:17
  188.2 4.2 copy-start.15
  188.2 5.2 copy-start.17
  188.2 6.3 copy-start.19
  191.9 13.2 collective-permute-start.8
  195.6 11.6 copy-start.13
  247.0 2.0 copy-start.1
  355.7 11.3 copy-start.20
  355.7 24.0 %slice-start = ((s8[8388608]{0:T(1024)(128)(4,1)}), s8[4194304]{0:T(1024)(128)(4,1)S(1)}, s32[]{:S(2)}) async-start(s8[8388608]{0:T(1024)(128)(4,1)} %bitcast.266), calls=%async_computation.22 | async-start | bytes 8388608
  367.0 12.7 slice-start.1
  379.6 6.9 copy-start.39
  396.4 242.7 %all-reduce.11.cloned.1.call-start = ((), (), s32[]{:S(2)}) async-start(), calls=%async_computation.12 | async-start | bytes 4194304 | tf_op jit(solution)/shard_map/psum | solution.py:206
  406.3 430.2 %all-reduce.15.cloned.1.call-start = ((), (), s32[]{:S(2)}) async-start(), calls=%async_computation.14 | async-start | bytes 8388608 | tf_op jit(solution)/shard_map/psum | solution.py:237
  639.1 10.1 copy-start.22
  647.2 2.0 copy-start.4
  647.2 3.3 copy-start.29
  650.5 24.5 %copy-start.24 = (f32[512,32]{0,1:T(8,128)S(1)}, f32[512,32]{0,1:T(8,128)}, u32[]{:S(2)}) copy-start(f32[512,32]{0,1:T(8,128)} %copy-done.23) | copy-start | bytes 196612
  650.5 24.5 %copy-start.27 = (f32[512,32]{0,1:T(8,128)S(1)}, f32[512,32]{0,1:T(8,128)}, u32[]{:S(2)}) copy-start(f32[512,32]{0,1:T(8,128)} %get-tuple-element.232) | copy-start | bytes 196612
  651.9 3.3 copy-start.25
  662.1 3.3 copy-start.25
  670.9 5.5 copy-start.6
  672.1 6.5 collective-permute-start.10
  673.5 4.3 collective-permute-start.9
  676.4 1.5 copy-start.8
  677.8 1.0 copy-start.10
  681.6 3.6 copy-start.3
  681.6 193.7 %reduce-scatter.12.cloned.1.call-start = ((), (), s32[]{:S(2)}) async-start(), calls=%async_computation.17 | async-start | bytes 1179648 | tf_op jit(solution)/shard_map/reduce_scatter | solution.py:243
  685.2 229.7 %reduce-scatter.10.cloned.1.call-start = ((), (), s32[]{:S(2)}) async-start(), calls=%async_computation.16 | async-start | bytes 1179648 | tf_op jit(solution)/shard_map/reduce_scatter | solution.py:242
  687.0 283.0 %reduce-scatter.14.cloned.1.call-start = ((), (), s32[]{:S(2)}) async-start(), calls=%async_computation.18 | async-start | bytes 4718592 | tf_op jit(solution)/shard_map/reduce_scatter | solution.py:244
  692.7 332.2 %reduce-scatter.8.cloned.1.call-start = ((), (), s32[]{:S(2)}) async-start(), calls=%async_computation.15 | async-start | bytes 4718592 | tf_op jit(solution)/shard_map/reduce_scatter | solution.py:241
  696.1 1.6 copy-start.21
  696.1 449.1 %reduce-scatter.16.cloned.1.call-start = ((), (), s32[]{:S(2)}) async-start(), calls=%async_computation.19 | async-start | bytes 18874368 | tf_op jit(solution)/shard_map/reduce_scatter | solution.py:245
  707.5 558.0 %reduce-scatter.18.cloned.1.call-start = ((), (), s32[]{:S(2)}) async-start(), calls=%async_computation.20 | async-start | bytes 18874368 | tf_op jit(solution)/shard_map/reduce_scatter | solution.py:246
  717.5 1.6 copy-start.38
  717.5 668.0 %reduce-scatter.20.cloned.1.call-start = ((), (), s32[]{:S(2)}) async-start(), calls=%async_computation.21 | async-start | bytes 18874368 | tf_op jit(solution)/shard_map/reduce_scatter | solution.py:247
  729.5 107.0 %copy-start.31 = (f32[8,1,256]{2,1,0:T(1,128)S(1)}, f32[8,1,256]{2,1,0:T(1,128)}, u32[]{:S(2)}) copy-start(f32[8,1,256]{2,1,0:T(1,128)} %copy-done.30) | copy-start | bytes 24580
  729.5 107.0 %copy-start.34 = (f32[512]{0:T(512)S(1)}, f32[512]{0:T(512)}, u32[]{:S(2)}) copy-start(f32[512]{0:T(512)} %copy-done.33) | copy-start | bytes 6148
  731.4 135.0 %copy-start.35 = (f32[512]{0:T(512)S(1)}, f32[512]{0:T(512)}, u32[]{:S(2)}) copy-start(f32[512]{0:T(512)} %get-tuple-element.235) | copy-start | bytes 6148
  (7 other events, 6.5 us)
Sparse Core Ops, SparseCore 0:
  9.9 31.1 all-gather.6
  54.6 28.3 all-gather.8
  88.0 154.9 all-reduce.8
  244.8 53.2 all-gather.10
  299.8 55.8 all-gather.12
  396.5 155.0 all-reduce.12
  553.9 85.0 all-reduce.10
  681.7 154.7 all-reduce.14
  840.3 34.9 reduce-scatter.11
  878.9 35.9 reduce-scatter.9
  918.8 51.0 reduce-scatter.13
  973.7 51.1 reduce-scatter.7
  1029.0 116.1 reduce-scatter.15
  1149.3 116.1 reduce-scatter.17
  1269.5 115.9 reduce-scatter.19
